TPU v7x, 32 devices: a whole 2x2x4 slice. The times are simulated.
32 devices in a mesh: wide: 4 (over z), narrow: 8 (over y, x, core).
Axes of the slice: x: 2, y: 2, z: 4, core: 2. Of those that a mesh axis runs over, the one named last changes fastest.
Arguments:
- phase_ids: int32 [512, 512, 256], P('wide', 'narrow'), may hold values from 0 to 3
- conduct_table: float32 [4, 3], replicated, may hold values from 0.2 to 5
- gradient: float32 [3], replicated, may hold values from -3 to 3
- start_field: float32 [512, 512, 256], P('wide', 'narrow'), may hold values from -32 to 32
Outputs:
- solution: float32 [512, 512, 256], P('wide', 'narrow')
- residual_next: float32 [512, 512, 256], P('wide', 'narrow')
- new_direction: float32 [512, 512, 256], P('wide', 'narrow')
Inputs may be any that keep to these rules, and one draw needn't show every extreme that they name: `phase_ids`: each voxel's phase indexes a row of conduct_table.
All inputs are finite; a program needn't handle non-finite values.
Results may differ from a plain program's by a relative error of at most 0.0065.
Values sent between devices are 32-bit elements; how exact they have to be, the bound alone decides.
No kernel may reach another device: no remote copies, remote signals or barrier semaphores. Data moves between devices by JAX's collectives and lax.ppermute only.
A program may use at most 256 MiB of HBM per device.

v0:
```python
import jax
import jax.numpy as jnp
from jax import lax
from jax.sharding import PartitionSpec as P

NX = 512
NY = 512
NZ = 256
PHASES = 4
HIGHEST = lax.Precision.HIGHEST
FORWARD_FORMS = ("nyz,mn->myz", "xnz,mn->xmz", "xyn,mn->xym")
INVERSE_FORMS = ("myz,mn->nyz", "xmz,mn->xnz", "xym,mn->xyn")


def extended(shard, sides, width):
    for axis, dim in sides:
        devices, length = (lax.axis_size(axis), shard.shape[dim])
        up = [(i, (i + 1) % devices) for i in range(devices - 1)]
        down = [(j, i) for i, j in up]
        last = lax.slice_in_dim(shard, length - width, length, axis=dim)
        initial = lax.slice_in_dim(shard, 0, width, axis=dim)
        before = lax.ppermute(last, axis, up)
        after = lax.ppermute(initial, axis, down)
        shard = jnp.concatenate([before, shard, after], axis=dim)
    return shard


def cosine_table(length):
    freq_index = jnp.arange(length, dtype=jnp.int32)[:, None]
    cell_index = jnp.arange(length, dtype=jnp.int32)[None, :]
    wrapped = freq_index * (2 * cell_index + 1) % (4 * length)
    angle_rad = wrapped.astype(jnp.float32) * (jnp.pi / (2.0 * length))
    weight = jnp.where(
        freq_index == 0, jnp.sqrt(jnp.float32(1.0 / length)), jnp.sqrt(jnp.float32(2.0 / length))
    )
    return weight * jnp.cos(angle_rad)


def eigen_values(length, index):
    angle_rad = index.astype(jnp.float32) * (jnp.pi / length)
    return 2.0 - 2.0 * jnp.cos(angle_rad)


def green_block(base_cond, index_x, index_y, index_z):
    lowest = eigen_values(NX, jnp.ones((), jnp.int32))
    eigen_sum = lowest + eigen_values(NX, index_x)[:, None, None]
    eigen_sum = eigen_sum + eigen_values(NY, index_y)[None, :, None]
    eigen_sum = eigen_sum + eigen_values(NZ, index_z)[None, None, :]
    zero_mode = (
        (index_x[:, None, None] == 0)
        & (index_y[None, :, None] == 0)
        & (index_z[None, None, :] == 0)
    )
    return jnp.where(zero_mode, jnp.float32(0.0), 1.0 / (base_cond * eigen_sum))


def transform(values, matrix, axis_dim, inverse):
    einsum_form = INVERSE_FORMS[axis_dim] if inverse else FORWARD_FORMS[axis_dim]
    return jnp.einsum(einsum_form, values, matrix, precision=HIGHEST)


def harmonic(lower_side, upper_side):
    return 2.0 * lower_side * upper_side / (lower_side + upper_side)


def conductivities(phase_ids, conduct_table):
    result = []
    for component in range(3):
        summed = jnp.zeros(phase_ids.shape, jnp.float32)
        for member in range(PHASES):
            summed = summed + jnp.where(
                phase_ids == member, conduct_table[member, component], jnp.float32(0.0)
            )
        result.append(summed)
    return result


def pad_depth(values):
    return jnp.pad(values, ((0, 0), (0, 0), (1, 1)))


def apply_padded(field_pad, faces):
    inner_x = field_pad[:, 1:-1, :]
    flux_x = faces[0] * (inner_x[1:] - inner_x[:-1])
    inner_y = field_pad[1:-1, :, :]
    flux_y = faces[1] * (inner_y[:, 1:] - inner_y[:, :-1])
    inner_z = pad_depth(field_pad[1:-1, 1:-1, :])
    flux_z = faces[2] * (inner_z[:, :, 1:] - inner_z[:, :, :-1])
    divergence = flux_x[1:] - flux_x[:-1] + (flux_y[:, 1:] - flux_y[:, :-1])
    divergence = divergence + (flux_z[:, :, 1:] - flux_z[:, :, :-1])
    return -divergence


def precondition(grid_field, tables, base_cond):
    table_x, table_y, table_z = tables
    spectral = transform(grid_field, table_z, 2, False)
    spectral = transform(
        lax.all_to_all(spectral, "narrow", split_axis=2, concat_axis=1, tiled=True),
        table_y,
        1,
        False,
    )
    spectral = transform(
        lax.all_to_all(spectral, "wide", split_axis=1, concat_axis=0, tiled=True), table_x, 0, False
    )
    count_y = spectral.shape[1]
    count_z = spectral.shape[2]
    index_x = jnp.arange(NX, dtype=jnp.int32)
    index_y = lax.axis_index("wide") * count_y + jnp.arange(count_y, dtype=jnp.int32)
    index_z = lax.axis_index("narrow") * count_z + jnp.arange(count_z, dtype=jnp.int32)
    spectral = spectral * green_block(base_cond, index_x, index_y, index_z)
    spectral = transform(spectral, table_x, 0, True)
    spectral = transform(
        lax.all_to_all(spectral, "wide", split_axis=0, concat_axis=1, tiled=True), table_y, 1, True
    )
    return transform(
        lax.all_to_all(spectral, "narrow", split_axis=1, concat_axis=2, tiled=True),
        table_z,
        2,
        True,
    )


def on_device(phase_ids, conduct_table, gradient, start_field):
    cond_x, cond_y, cond_z = conductivities(phase_ids, conduct_table)
    stacked = jnp.stack([start_field, cond_x, cond_y])
    padded = extended(stacked, (("wide", 1), ("narrow", 2)), 1)
    start_pad = padded[0]
    cond_xp = padded[1][:, 1:-1, :]
    cond_yp = padded[2][1:-1, :, :]
    cond_zp = pad_depth(cond_z)
    faces = (
        harmonic(cond_xp[:-1], cond_xp[1:]),
        harmonic(cond_yp[:, :-1], cond_yp[:, 1:]),
        harmonic(cond_zp[:, :, :-1], cond_zp[:, :, 1:]),
    )
    source = gradient[0] * (faces[0][1:] - faces[0][:-1])
    source = source + gradient[1] * (faces[1][:, 1:] - faces[1][:, :-1])
    source = source + gradient[2] * (faces[2][:, :, 1:] - faces[2][:, :, :-1])
    residual = source - apply_padded(start_pad, faces)
    tables = (cosine_table(NX), cosine_table(NY), cosine_table(NZ))
    base_cond = jnp.mean(conduct_table)
    direction = precondition(residual, tables, base_cond)
    direction_pad = extended(direction, (("wide", 0), ("narrow", 1)), 1)
    image_field = apply_padded(direction_pad, faces)
    rz_now = lax.psum(jnp.sum(residual * direction), ("wide", "narrow"))
    curvature = lax.psum(jnp.sum(direction * image_field), ("wide", "narrow"))
    step_alpha = rz_now / curvature
    solution = start_field + step_alpha * direction
    residual_next = residual - step_alpha * image_field
    preconditioned = precondition(residual_next, tables, base_cond)
    rz_next = lax.psum(jnp.sum(residual_next * preconditioned), ("wide", "narrow"))
    new_direction = preconditioned + rz_next / rz_now * direction
    return (solution, residual_next, new_direction)


def solution(mesh):
    placed = (P("wide", "narrow", None), P(), P(), P("wide", "narrow", None))
    return jax.shard_map(
        on_device,
        mesh=mesh,
        in_specs=placed,
        out_specs=(P("wide", "narrow", None), P("wide", "narrow", None), P("wide", "narrow", None)),
        check_vma=False,
    )
```

profile of v0, /device:TPU:0, one launch (start us, length us, event | category | flops | bytes accessed | tf_op | source)
XLA Modules:
  0.0 1928.2 jit_solution(9255614372349274259)
XLA Ops:
  2.4 8.4 copy.155
  10.8 14.0 add_bitcast_fusion.1
  24.8 14.6 select_add_fusion
  59.9 10.3 pad_maximum_fusion
  70.2 11.6 slice_bitcast_fusion.3
  81.7 10.8 slice_bitcast_fusion.1
  98.6 19.2 fusion.4
  117.8 19.0 fusion.8
  136.8 22.0 %fusion.1 = (f32[128,64,257]{2,0,1:T(8,128)}, f32[128,64,257]{2,0,1:T(8,128)}) fusion(f32[128,64,256]{2,0,1:T(8,128)} %slice.296, f32[128,64,256]{2,0,1:T(8,128)} %get-tuple-element.45), kind=kLoop, calls=%fused_computation.8 | loop fusion | flops 12632064 | bytes 33619968 | tf_op jit(solution)/shard_map/mul | solution.py:88
  158.8 41.1 %fusion.14 = f32[128,64,256]{2,0,1:T(8,128)} fusion(f32[128,64,257]{2,0,1:T(8,128)} %get-tuple-element.24, f32[128,65,256]{2,0,1:T(8,128)} %get-tuple-element.22, f32[129,64,256]{2,0,1:T(8,128)} %get-tuple-element.20, f32[128,64,257]{2,0,1:T(8,128)} %get-tuple-element.25, f32[128,65,256]{2,0,1:T(8,128)} %get-tuple-element.23, ...), kind=kLoop, calls=%fused_computation.41 | loop fusion | flops 31457280 | bytes 109051920 | tf_op jit(solution)/shard_map/sub | solution.py:140
  199.9 13.0 fusion.131
  213.0 8.7 copy.87
  221.6 10.1 all-to-all-start
  231.8 94.1 %all-to-all-done = f32[128,64,256]{0,1,2:T(8,128)} async-done(((f32[128,64,256]{0,1,2:T(8,128)}), f32[128,64,256]{0,1,2:T(8,128)}, u32[]{:S(2)}, u32[]{:S(2)}) %all-to-all-start) | async-done | bytes 8388640 | tf_op jit(solution)/shard_map/all_to_all | solution.py:98
  334.1 29.1 %fusion.43 = f32[128,512,32]{0,1,2:T(8,128)S(1)} fusion(f32[128,512,32]{0,2,1:T(8,128)S(1)} %bitcast.111, s32[512]{0:T(512)S(1)} %multiply_add_fusion.2, f32[512]{0:T(512)S(1)} %broadcast_select_fusion), kind=kOutput, calls=%fused_computation.92 | convolution fusion | flops 12888834048 | bytes 16781312 | tf_op jit(solution)/shard_map/xnz,mn->xmz/dot_general | solution.py:59
  363.2 8.3 copy.92
  379.0 179.1 %all-to-all-done.1 = f32[128,512,32]{0,2,1:T(8,128)} async-done(((f32[128,512,32]{0,2,1:T(8,128)}), f32[128,512,32]{0,2,1:T(8,128)}, u32[]{:S(2)}, u32[]{:S(2)}) %all-to-all-start.1) | async-done | bytes 8388640 | tf_op jit(solution)/shard_map/all_to_all | solution.py:104
  558.1 9.9 copy.128
  568.0 22.5 %fusion.62 = f32[512,128,32]{1,0,2:T(8,128)S(1)} fusion(f32[512,128,32]{1,0,2:T(8,128)} %bitcast.109, s32[512]{0:T(512)S(1)} %multiply_add_fusion.2, f32[512]{0:T(512)S(1)} %broadcast_select_fusion), kind=kOutput, calls=%fused_computation.109 | convolution fusion | flops 12888834048 | bytes 16781312 | tf_op jit(solution)/shard_map/nyz,mn->myz/dot_general | solution.py:59
  590.5 20.1 %fusion.27 = f32[512,128,32]{1,0,2:T(8,128)S(1)} fusion(f32[512,128,32]{1,0,2:T(8,128)S(1)} %fusion.62, f32[32]{0:T(128)S(1)} %multiply_subtract_fusion.2, f32[512,128]{1,0:T(8,128)S(1)} %broadcast_add_fusion, f32[]{:T(128)S(6)} %div.25, pred[512,128]{1,0:T(8,128)(4,1)S(1)} %broadcast_and_fusion, pred[32]{0:T(512)(128)(4,1)S(1)} %fusion.157, ...), kind=kOutput, calls=%fused_computation.67 | convolution fusion | flops 12901416960 | bytes 17109156 | tf_op jit(solution)/shard_map/myz,mn->nyz/dot_general | solution.py:59
  615.5 186.7 %all_to_all.144 = f32[512,128,32]{1,2,0:T(8,128)} all-to-all(f32[512,128,32]{1,2,0:T(8,128)S(1)} %copy.96), channel_id=1, replica_groups=mesh['wide'=4,'narrow'=8] {'wide'}, dimensions={0} | all-to-all | bytes 16777216 | tf_op jit(solution)/shard_map/all_to_all | solution.py:114
  802.1 12.2 copy.154
  814.3 10.3 all_to_all.115
  824.6 24.8 %convolution_bitcast_fusion.1 = f32[128,512,32]{0,1,2:T(8,128)S(1)} fusion(f32[128,512,32]{1,0,2:T(8,128)} %all_to_all.115, s32[512]{0:T(512)S(1)} %multiply_add_fusion.2, f32[512]{0:T(512)S(1)} %broadcast_select_fusion), kind=kOutput, calls=%fused_computation.95 | convolution fusion | flops 12888834048 | bytes 16781312 | tf_op jit(solution)/shard_map/xmz,mn->xnz/dot_general | solution.py:59
  854.3 98.0 %all_to_all.145 = f32[128,512,32]{0,2,1:T(8,128)S(1)} all-to-all(f32[128,512,32]{0,2,1:T(8,128)S(1)} %copy.98), channel_id=1, replica_groups=mesh['wide'=4,'narrow'=8] {'narrow'}, dimensions={1} | all-to-all | bytes 16777216 | tf_op jit(solution)/shard_map/all_to_all | solution.py:117
  956.8 18.2 fusion.129
  978.5 10.8 fusion.3
  1008.0 25.2 %multiply_reduce_fusion.1 = (f32[]{:T(128)}, f32[]{:T(128)}, f32[128,64,256]{2,0,1:T(8,128)}) fusion(f32[128,64,256]{2,0,1:T(8,128)S(1)} %fusion.129, f32[128,64,256]{2,0,1:T(8,128)} %fusion.14, f32[128,64,257]{2,0,1:T(8,128)} %fusion.3, f32[128,65,256]{2,0,1:T(8,128)} %fusion.7, f32[129,64,256]{2,0,1:T(8,128)} %fusion.5), kind=kLoop, calls=%fused_computation.65 | loop fusion | flops 20971520 | bytes 75497480 | tf_op jit(solution)/shard_map/reduce_sum | solution.py:147
  1033.1 40.6 %all-reduce.3 = (f32[]{:T(128)}, f32[]{:T(128)}) all-reduce(f32[]{:T(128)} %get-tuple-element.16, f32[]{:T(128)} %get-tuple-element.15), channel_id=1, replica_groups=mesh['wide'=4,'narrow'=8] {'wide','narrow'}, use_global_device_ids=true, to_apply=%region_2.3 | all-reduce | flops 2 | bytes 16 | tf_op jit(solution)/shard_map/psum | solution.py:146
  1075.0 11.6 multiply_subtract_fusion
  1086.6 13.0 fusion.127
  1099.7 8.7 copy.102
  1108.3 97.8 %all_to_all.146 = f32[128,64,256]{0,1,2:T(8,128)S(1)} all-to-all(f32[128,64,256]{0,1,2:T(8,128)} %copy.102), channel_id=1, replica_groups=mesh['wide'=4,'narrow'=8] {'narrow'}, dimensions={2} | all-to-all | bytes 16777216 | tf_op jit(solution)/shard_map/all_to_all | solution.py:98
  1210.9 29.1 %fusion.46 = f32[128,512,32]{0,1,2:T(8,128)S(1)} fusion(f32[128,512,32]{0,2,1:T(8,128)S(1)} %bitcast.112, s32[512]{0:T(512)S(1)} %multiply_add_fusion.2, f32[512]{0:T(512)S(1)} %broadcast_select_fusion), kind=kOutput, calls=%fused_computation.93 | convolution fusion | flops 12888834048 | bytes 16781312 | tf_op jit(solution)/shard_map/xnz,mn->xmz/dot_general | solution.py:59
  1244.9 186.4 %all_to_all.147 = f32[128,512,32]{0,2,1:T(8,128)} all-to-all(f32[128,512,32]{0,2,1:T(8,128)S(1)} %copy.107), channel_id=1, replica_groups=mesh['wide'=4,'narrow'=8] {'wide'}, dimensions={1} | all-to-all | bytes 16777216 | tf_op jit(solution)/shard_map/all_to_all | solution.py:104
  1431.3 9.9 copy.132
  1441.2 22.5 %fusion.59 = f32[512,128,32]{1,0,2:T(8,128)S(1)} fusion(f32[512,128,32]{1,0,2:T(8,128)} %bitcast.110, s32[512]{0:T(512)S(1)} %multiply_add_fusion.2, f32[512]{0:T(512)S(1)} %broadcast_select_fusion), kind=kOutput, calls=%fused_computation.108 | convolution fusion | flops 12888834048 | bytes 16781312 | tf_op jit(solution)/shard_map/nyz,mn->myz/dot_general | solution.py:59
  1463.7 20.1 %fusion.25 = f32[512,128,32]{1,0,2:T(8,128)S(1)} fusion(f32[512,128,32]{1,0,2:T(8,128)S(1)} %fusion.59, f32[32]{0:T(128)S(1)} %multiply_subtract_fusion.2, f32[512,128]{1,0:T(8,128)S(1)} %broadcast_add_fusion, f32[]{:T(128)S(6)} %div.25, pred[512,128]{1,0:T(8,128)(4,1)S(1)} %broadcast_and_fusion, pred[32]{0:T(512)(128)(4,1)S(1)} %fusion.157, ...), kind=kOutput, calls=%fused_computation.61 | convolution fusion | flops 12901416960 | bytes 17109156 | tf_op jit(solution)/shard_map/myz,mn->nyz/dot_general | solution.py:59
  1488.7 185.9 %all_to_all.148 = f32[512,128,32]{1,2,0:T(8,128)} all-to-all(f32[512,128,32]{1,2,0:T(8,128)S(1)} %copy.111), channel_id=1, replica_groups=mesh['wide'=4,'narrow'=8] {'wide'}, dimensions={0} | all-to-all | bytes 16777216 | tf_op jit(solution)/shard_map/all_to_all | solution.py:114
  1674.6 12.2 copy.153
  1686.7 10.3 all_to_all.131
  1697.0 24.9 %convolution_bitcast_fusion = f32[128,512,32]{0,1,2:T(8,128)S(1)} fusion(f32[128,512,32]{1,0,2:T(8,128)} %all_to_all.131, s32[512]{0:T(512)S(1)} %multiply_add_fusion.2, f32[512]{0:T(512)S(1)} %broadcast_select_fusion), kind=kOutput, calls=%fused_computation.94 | convolution fusion | flops 12888834048 | bytes 16781312 | tf_op jit(solution)/shard_map/xmz,mn->xnz/dot_general | solution.py:59
  1735.1 11.6 copy.117
  1746.7 82.4 %all-to-all-done.7 = f32[128,512,32]{0,2,1:T(8,128)} async-done(((f32[128,512,32]{0,2,1:T(8,128)}), f32[128,512,32]{0,2,1:T(8,128)}, u32[]{:S(2)}, u32[]{:S(2)}) %all-to-all-start.7) | async-done | bytes 8388640 | tf_op jit(solution)/shard_map/all_to_all | solution.py:117
  1833.6 21.2 %multiply_reduce_fusion = (f32[]{:T(128)}, f32[128,64,256]{2,0,1:T(8,128)}) fusion(f32[128,64,256]{2,0,1:T(8,128)} %multiply_subtract_fusion, f32[128,64,256]{0,2,1:T(8,128)S(1)} %bitcast.113, s32[256]{0:T(256)S(1)} %multiply_add_fusion.3, f32[256]{0:T(256)S(1)} %compare_select_fusion), kind=kOutput, calls=%fused_computation.60 | convolution fusion | flops 6447628288 | bytes 25167876 | tf_op jit(solution)/shard_map/xym,mn->xyn/dot_general | solution.py:59
  1854.8 38.1 %psum.23 = f32[]{:T(128)} all-reduce(f32[]{:T(128)} %get-tuple-element.62), channel_id=1, replica_groups=mesh['wide'=4,'narrow'=8] {'wide','narrow'}, use_global_device_ids=true, to_apply=%region_6.7 | all-reduce | flops 1 | bytes 8 | tf_op jit(solution)/shard_map/psum | solution.py:152
  1894.1 13.9 multiply_add_fusion
  1908.0 11.6 copy.118
  (60 shorter events, 119.8 us)
Async XLA Ops:
  2.4 8.4 copy-start.2
  39.8 9.1 collective-permute-start
  44.7 11.2 copy-start.4
  44.7 8.3 collective-permute-start.1
  53.1 3.4 collective-permute-start.2
  54.6 5.4 collective-permute-start.3
  92.6 6.1 copy-start.1
  221.6 104.3 %all-to-all-start = ((f32[128,64,256]{0,1,2:T(8,128)}), f32[128,64,256]{0,1,2:T(8,128)}, u32[]{:S(2)}, u32[]{:S(2)}) async-start(f32[128,64,256]{0,1,2:T(8,128)} %copy.87), calls=%async_computation | async-start | bytes 16777216 | tf_op jit(solution)/shard_map/all_to_all | solution.py:98
  371.5 5.8 copy-start.3
  371.5 186.6 %all-to-all-start.1 = ((f32[128,512,32]{0,2,1:T(8,128)}), f32[128,512,32]{0,2,1:T(8,128)}, u32[]{:S(2)}, u32[]{:S(2)}) async-start(f32[128,512,32]{0,2,1:T(8,128)} %copy.92), calls=%async_computation.1 | async-start | bytes 16777216 | tf_op jit(solution)/shard_map/all_to_all | solution.py:104
  974.9 33.0 %copy-start = (f32[128,64,256]{2,0,1:T(8,128)}, f32[128,64,256]{2,0,1:T(8,128)S(1)}, u32[]{:S(2)}) copy-start(f32[128,64,256]{2,0,1:T(8,128)S(1)} %fusion.129) | copy-start | bytes 25165828
  975.1 14.2 collective-permute-start.5
  977.2 12.1 collective-permute-start.4
  989.3 11.6 collective-permute-start.6
  990.6 10.3 collective-permute-start.7
  1730.1 99.0 %all-to-all-start.7 = ((f32[128,512,32]{0,2,1:T(8,128)}), f32[128,512,32]{0,2,1:T(8,128)}, u32[]{:S(2)}, u32[]{:S(2)}) async-start(f32[128,512,32]{0,2,1:T(8,128)} %copy.113), calls=%async_computation.7 | async-start | bytes 16777216 | tf_op jit(solution)/shard_map/all_to_all | solution.py:117
where the time goes:
time: 1940 us; the launch traced here: 1930 us
  blocking collectives  834 us (43%)
  waiting for transfers between devices  366 us (19%)
  matrix products  259 us (13%)
  other arithmetic  217 us (11%)
  local copies, waits for them, and re-layouts  210 us (11%)
  starting transfers between devices  37.6 us (2%)
    all_to_all x2, blocking collectives, precondition(): lax.all_to_all(spectral, 'wide', split_axis=0, concat_axis=1, tiled=True)  373 us
    dot_general x12, matrix products, transform(): return jnp.einsum(einsum_form, values, matrix, precision=HIGHEST)  259 us
    all_to_all x1, blocking collectives, precondition(): lax.all_to_all(spectral, 'wide', split_axis=1, concat_axis=0, tiled=True)  186 us
    all_to_all x1, waiting for transfers between devices, precondition(): lax.all_to_all(spectral, 'wide', split_axis=1, concat_axis=0, tiled=True)  179 us
    all_to_all x1, blocking collectives, precondition(): lax.all_to_all(spectral, 'narrow', split_axis=1, concat_axis=2, tiled=True)  98 us
    all_to_all x1, blocking collectives, precondition(): lax.all_to_all(spectral, 'narrow', split_axis=2, concat_axis=1, tiled=True)  97.8 us
    all_to_all x1, waiting for transfers between devices, precondition(): lax.all_to_all(spectral, 'narrow', split_axis=2, concat_axis=1, tiled=True)  94.1 us
    all_to_all x1, waiting for transfers between devices, precondition(): lax.all_to_all(spectral, 'narrow', split_axis=1, concat_axis=2, tiled=True)  82.4 us
  transfers between devices with their start and end apart: 11, of which 6 were waited for; matrix products, arithmetic and copies ran while one was open for 2% of the time, Pallas kernels for 0%

commit v1 on v0

--- a/solution.py
+++ b/solution.py
@@ -10,6 +10,29 @@
 HIGHEST = lax.Precision.HIGHEST
 FORWARD_FORMS = ("nyz,mn->myz", "xnz,mn->xmz", "xyn,mn->xym")
 INVERSE_FORMS = ("myz,mn->nyz", "xmz,mn->xnz", "xym,mn->xyn")
+
+
+def cut_along(x, dim, peers):
+    shape = x.shape
+    pieces = x.reshape(*shape[:dim], peers, shape[dim] // peers, *shape[dim + 1 :])
+    return jnp.moveaxis(pieces, dim, 0)
+
+
+def laid_out(blocks, dim):
+    blocks = jnp.moveaxis(blocks, 0, dim)
+    dims = blocks.shape
+    return blocks.reshape(*dims[:dim], dims[dim] * dims[dim + 1], *dims[dim + 2 :])
+
+
+def rotated_exchange(x, axis, split_dim, concat_dim):
+    size, mine = (lax.axis_size(axis), lax.axis_index(axis))
+    blocks = cut_along(x, split_dim, size)
+    done = [blocks[mine]]
+    for hop in range(1, size):
+        sent = blocks[(mine + hop) % size]
+        done.append(lax.ppermute(sent, axis, [(i, (i + hop) % size) for i in range(size)]))
+    blocks = jnp.stack(done)[(mine - jnp.arange(size)) % size]
+    return laid_out(blocks, concat_dim)
 
 
 def extended(shard, sides, width):
@@ -94,12 +117,7 @@
 def precondition(grid_field, tables, base_cond):
     table_x, table_y, table_z = tables
     spectral = transform(grid_field, table_z, 2, False)
-    spectral = transform(
-        lax.all_to_all(spectral, "narrow", split_axis=2, concat_axis=1, tiled=True),
-        table_y,
-        1,
-        False,
-    )
+    spectral = transform(rotated_exchange(spectral, "narrow", 2, 1), table_y, 1, False)
     spectral = transform(
         lax.all_to_all(spectral, "wide", split_axis=1, concat_axis=0, tiled=True), table_x, 0, False
     )

time: 1940 us -> 1950 us (level)
  blocking collectives: 834 us -> 739 us
  waiting for transfers between devices: 366 us -> 422 us
  starting transfers between devices: 37.6 us -> 58 us
    ppermute x0 -> x14, waiting for transfers between devices: none -> 147 us  [rotated_exchange(): lax.ppermute(sent, axis, [(i, (i + hop) % size) for i in range(size)])]
    all_to_all x1 -> x0, blocking collectives: 97.8 us -> none  [precondition(): lax.all_to_all(spectral, 'narrow', split_axis=2, concat_axis=1, tiled=True)]
    all_to_all x1 -> x0, waiting for transfers between devices: 94.1 us -> none  [precondition(): lax.all_to_all(spectral, 'narrow', split_axis=2, concat_axis=1, tiled=True)]
    ppermute x0 -> x14, starting transfers between devices: none -> 30.8 us  [rotated_exchange(): lax.ppermute(sent, axis, [(i, (i + hop) % size) for i in range(size)])]
    unnamed x14 -> x54, local copies, waits for them, and re-layouts: 40.8 us -> 63.7 us
  transfers between devices with their start and end apart: 11 -> 24, of which waited for: 6 -> 14; matrix products, arithmetic and copies ran while one was open for 2% -> 3% of each run, Pallas kernels for 0% -> 0%
where the time goes in v1:
time: 1950 us; the launch traced here: 1940 us
  blocking collectives  739 us (38%)
  waiting for transfers between devices  422 us (22%)
  matrix products  265 us (14%)
  other arithmetic  227 us (12%)
  local copies, waits for them, and re-layouts  225 us (12%)
  starting transfers between devices  58 us (3%)
    all_to_all x2, blocking collectives, precondition(): lax.all_to_all(spectral, 'wide', split_axis=0, concat_axis=1, tiled=True)  375 us
    dot_general x12, matrix products, transform(): return jnp.einsum(einsum_form, values, matrix, precision=HIGHEST)  265 us
    all_to_all x1, blocking collectives, precondition(): lax.all_to_all(spectral, 'wide', split_axis=1, concat_axis=0, tiled=True)  189 us
    all_to_all x1, waiting for transfers between devices, precondition(): lax.all_to_all(spectral, 'wide', split_axis=1, concat_axis=0, tiled=True)  183 us
    ppermute x14, waiting for transfers between devices, rotated_exchange(): lax.ppermute(sent, axis, [(i, (i + hop) % size) for i in range(size)])  147 us
    all_to_all x1, blocking collectives, precondition(): lax.all_to_all(spectral, 'narrow', split_axis=1, concat_axis=2, tiled=True)  97.5 us
    all_to_all x1, waiting for transfers between devices, precondition(): lax.all_to_all(spectral, 'narrow', split_axis=1, concat_axis=2, tiled=True)  82.4 us
    unnamed x54, local copies, waits for them, and re-layouts  63.7 us
  transfers between devices with their start and end apart: 24, of which 14 were waited for; matrix products, arithmetic and copies ran while one was open for 3% of the time, Pallas kernels for 0%

profile of v1, /device:TPU:0, one launch (start us, length us, event | category | flops | bytes accessed | tf_op | source)
XLA Modules:
  0.0 1942.2 jit_solution(2127873021242847566)
XLA Ops:
  2.4 8.4 copy.143
  10.9 14.0 add_bitcast_fusion.1
  24.9 14.4 select_add_fusion
  59.7 20.4 %pad_maximum_fusion = f32[3,130,66,256]{3,1,2,0:T(8,128)} fusion(f32[3,130,1,256]{3,1,2,0:T(8,128)S(1)} %collective-permute-done.3, f32[3,1,64,256]{3,1,2,0:T(1,128)S(1)} %collective-permute-done.1, f32[1,128,64,256]{3,1,2,0:T(8,128)} %copy-done.4, f32[1,128,64,256]{3,1,2,0:T(8,128)} %copy-done.2, f32[1,128,64,256]{3,1,2,0:T(8,128)} %bitcast.172, ...), kind=kLoop, calls=%fused_computation.2 | loop fusion | flops 39536640 | bytes 52715520 | tf_op jit(solution)/shard_map/concatenate | solution.py:47
  80.1 11.6 slice_bitcast_fusion.3
  91.6 10.9 slice_bitcast_fusion.1
  108.6 19.1 fusion.4
  127.7 19.2 fusion.8
  146.8 22.0 %fusion.1 = (f32[128,64,257]{2,0,1:T(8,128)}, f32[128,64,257]{2,0,1:T(8,128)}) fusion(f32[128,64,256]{2,0,1:T(8,128)} %slice.300, f32[128,64,256]{2,0,1:T(8,128)} %get-tuple-element.59), kind=kLoop, calls=%fused_computation.10 | loop fusion | flops 12632064 | bytes 33619968 | tf_op jit(solution)/shard_map/mul | solution.py:111
  168.8 41.1 %fusion.14 = f32[128,64,256]{2,0,1:T(8,128)} fusion(f32[128,64,257]{2,0,1:T(8,128)} %get-tuple-element.24, f32[128,65,256]{2,0,1:T(8,128)} %get-tuple-element.22, f32[129,64,256]{2,0,1:T(8,128)} %get-tuple-element.20, f32[128,64,257]{2,0,1:T(8,128)} %get-tuple-element.25, f32[128,65,256]{2,0,1:T(8,128)} %get-tuple-element.23, ...), kind=kLoop, calls=%fused_computation.43 | loop fusion | flops 31457280 | bytes 109051920 | tf_op jit(solution)/shard_map/sub | solution.py:158
  209.9 13.5 fusion.131
  247.9 11.6 collective-permute-start.8
  267.1 34.0 %collective-permute-done.6 = f32[128,64,32]{0,2,1:T(8,128)} collective-permute-done((f32[128,64,32]{0,2,1:T(8,128)}, f32[128,64,32]{0,2,1:T(8,128)}, u32[]{:S(2)}, u32[]{:S(2)}) %collective-permute-start.6) | collective-permute-done | bytes 1048608 | tf_op jit(solution)/shard_map/ppermute | solution.py:33
  307.5 21.2 %collective-permute-done.8 = f32[128,64,32]{0,2,1:T(8,128)S(1)} collective-permute-done((f32[128,64,32]{0,2,1:T(8,128)S(1)}, f32[128,64,32]{0,2,1:T(8,128)S(1)}, u32[]{:S(2)}, u32[]{:S(2)}) %collective-permute-start.8) | collective-permute-done | bytes 1048608 | tf_op jit(solution)/shard_map/ppermute | solution.py:33
  339.7 32.0 %fusion.43 = f32[128,512,32]{0,1,2:T(8,128)S(1)} fusion(f32[128,512,32]{0,2,1:T(8,128)} %bitcast.169, s32[512]{0:T(512)S(1)} %multiply_add_fusion.2, f32[512]{0:T(512)S(1)} %broadcast_select_fusion), kind=kOutput, calls=%fused_computation.94 | convolution fusion | flops 12888834048 | bytes 16781312 | tf_op jit(solution)/shard_map/xnz,mn->xmz/dot_general | solution.py:82
  387.5 182.5 %all-to-all-done = f32[128,512,32]{0,2,1:T(8,128)} async-done(((f32[128,512,32]{0,2,1:T(8,128)}), f32[128,512,32]{0,2,1:T(8,128)}, u32[]{:S(2)}, u32[]{:S(2)}) %all-to-all-start) | async-done | bytes 8388640 | tf_op jit(solution)/shard_map/all_to_all | solution.py:122
  570.0 9.9 copy.117
  579.9 22.7 %fusion.62 = f32[512,128,32]{1,0,2:T(8,128)S(1)} fusion(f32[512,128,32]{1,0,2:T(8,128)} %bitcast.177, s32[512]{0:T(512)S(1)} %multiply_add_fusion.2, f32[512]{0:T(512)S(1)} %broadcast_select_fusion), kind=kOutput, calls=%fused_computation.141 | convolution fusion | flops 12888834048 | bytes 16781312 | tf_op jit(solution)/shard_map/nyz,mn->myz/dot_general | solution.py:82
  602.7 19.9 %fusion.27 = f32[512,128,32]{1,0,2:T(8,128)S(1)} fusion(f32[512,128,32]{1,0,2:T(8,128)S(1)} %fusion.62, f32[32]{0:T(128)S(1)} %multiply_subtract_fusion.2, f32[512,128]{1,0:T(8,128)S(1)} %broadcast_add_fusion, f32[]{:T(128)S(6)} %div.25, pred[512,128]{1,0:T(8,128)(4,1)S(1)} %broadcast_and_fusion, pred[32]{0:T(512)(128)(4,1)S(1)} %fusion.171, ...), kind=kOutput, calls=%fused_computation.69 | convolution fusion | flops 12901416960 | bytes 17109156 | tf_op jit(solution)/shard_map/myz,mn->nyz/dot_general | solution.py:82
  627.5 187.3 %all_to_all.108 = f32[512,128,32]{1,2,0:T(8,128)} all-to-all(f32[512,128,32]{1,2,0:T(8,128)S(1)} %copy.86), channel_id=1, replica_groups=mesh['wide'=4,'narrow'=8] {'wide'}, dimensions={0} | all-to-all | bytes 16777216 | tf_op jit(solution)/shard_map/all_to_all | solution.py:132
  814.8 12.2 copy.142
  826.9 10.3 all_to_all.85
  837.2 24.9 %convolution_bitcast_fusion.1 = f32[128,512,32]{0,1,2:T(8,128)S(1)} fusion(f32[128,512,32]{1,0,2:T(8,128)} %all_to_all.85, s32[512]{0:T(512)S(1)} %multiply_add_fusion.2, f32[512]{0:T(512)S(1)} %broadcast_select_fusion), kind=kOutput, calls=%fused_computation.97 | convolution fusion | flops 12888834048 | bytes 16781312 | tf_op jit(solution)/shard_map/xmz,mn->xnz/dot_general | solution.py:82
  867.0 97.5 %all_to_all.109 = f32[128,512,32]{0,2,1:T(8,128)S(1)} all-to-all(f32[128,512,32]{0,2,1:T(8,128)S(1)} %copy.88), channel_id=1, replica_groups=mesh['wide'=4,'narrow'=8] {'narrow'}, dimensions={1} | all-to-all | bytes 16777216 | tf_op jit(solution)/shard_map/all_to_all | solution.py:135
  968.9 18.2 fusion.129
  990.3 10.8 fusion.3
  1019.9 25.2 %multiply_reduce_fusion.1 = (f32[]{:T(128)}, f32[]{:T(128)}, f32[128,64,256]{2,0,1:T(8,128)}) fusion(f32[128,64,256]{2,0,1:T(8,128)S(1)} %fusion.129, f32[128,64,256]{2,0,1:T(8,128)} %fusion.14, f32[128,64,257]{2,0,1:T(8,128)} %fusion.3, f32[128,65,256]{2,0,1:T(8,128)} %fusion.7, f32[129,64,256]{2,0,1:T(8,128)} %fusion.5), kind=kLoop, calls=%fused_computation.67 | loop fusion | flops 20971520 | bytes 75497480 | tf_op jit(solution)/shard_map/reduce_sum | solution.py:165
  1045.0 40.6 %all-reduce.3 = (f32[]{:T(128)}, f32[]{:T(128)}) all-reduce(f32[]{:T(128)} %get-tuple-element.16, f32[]{:T(128)} %get-tuple-element.15), channel_id=1, replica_groups=mesh['wide'=4,'narrow'=8] {'wide','narrow'}, use_global_device_ids=true, to_apply=%region_2.3 | all-reduce | flops 2 | bytes 16 | tf_op jit(solution)/shard_map/psum | solution.py:164
  1087.0 11.6 multiply_subtract_fusion
  1098.6 13.5 fusion.127
  1119.6 19.6 %collective-permute-done.15 = f32[128,64,32]{0,2,1:T(8,128)S(1)} collective-permute-done((f32[128,64,32]{0,2,1:T(8,128)S(1)}, f32[128,64,32]{0,2,1:T(8,128)S(1)}, u32[]{:S(2)}, u32[]{:S(2)}) %collective-permute-start.15) | collective-permute-done | bytes 1048608 | tf_op jit(solution)/shard_map/ppermute | solution.py:33
  1143.0 41.5 %collective-permute-done.17 = f32[128,64,32]{0,2,1:T(8,128)S(1)} collective-permute-done((f32[128,64,32]{0,2,1:T(8,128)S(1)}, f32[128,64,32]{0,2,1:T(8,128)S(1)}, u32[]{:S(2)}, u32[]{:S(2)}) %collective-permute-start.17) | collective-permute-done | bytes 1048608 | tf_op jit(solution)/shard_map/ppermute | solution.py:33
  1186.6 20.5 %collective-permute-done.19 = f32[128,64,32]{0,2,1:T(8,128)S(1)} collective-permute-done((f32[128,64,32]{0,2,1:T(8,128)S(1)}, f32[128,64,32]{0,2,1:T(8,128)S(1)}, u32[]{:S(2)}, u32[]{:S(2)}) %collective-permute-start.19) | collective-permute-done | bytes 1048608 | tf_op jit(solution)/shard_map/ppermute | solution.py:33
  1218.2 32.0 %fusion.46 = f32[128,512,32]{0,1,2:T(8,128)S(1)} fusion(f32[128,512,32]{0,2,1:T(8,128)} %bitcast.168, s32[512]{0:T(512)S(1)} %multiply_add_fusion.2, f32[512]{0:T(512)S(1)} %broadcast_select_fusion), kind=kOutput, calls=%fused_computation.95 | convolution fusion | flops 12888834048 | bytes 16781312 | tf_op jit(solution)/shard_map/xnz,mn->xmz/dot_general | solution.py:82
  1255.1 188.6 %all_to_all.110 = f32[128,512,32]{0,2,1:T(8,128)} all-to-all(f32[128,512,32]{0,2,1:T(8,128)S(1)} %copy.95), channel_id=1, replica_groups=mesh['wide'=4,'narrow'=8] {'wide'}, dimensions={1} | all-to-all | bytes 16777216 | tf_op jit(solution)/shard_map/all_to_all | solution.py:122
  1443.7 9.9 copy.120
  1453.6 22.5 %fusion.59 = f32[512,128,32]{1,0,2:T(8,128)S(1)} fusion(f32[512,128,32]{1,0,2:T(8,128)} %bitcast.178, s32[512]{0:T(512)S(1)} %multiply_add_fusion.2, f32[512]{0:T(512)S(1)} %broadcast_select_fusion), kind=kOutput, calls=%fused_computation.140 | convolution fusion | flops 12888834048 | bytes 16781312 | tf_op jit(solution)/shard_map/nyz,mn->myz/dot_general | solution.py:82
  1476.2 20.1 %fusion.25 = f32[512,128,32]{1,0,2:T(8,128)S(1)} fusion(f32[512,128,32]{1,0,2:T(8,128)S(1)} %fusion.59, f32[32]{0:T(128)S(1)} %copy-done.15, f32[512,128]{1,0:T(8,128)S(1)} %copy-done.8, f32[]{:T(128)S(6)} %div.25, pred[512,128]{1,0:T(8,128)(4,1)S(1)} %copy-done.10, pred[32]{0:T(512)(128)(4,1)S(1)} %copy-done.17, s32[512]{0:T(512)S(1)} %multiply_add_fusion.2, ...), kind=kOutput, calls=%fused_computation.63 | convolution fusion | flops 12901416960 | bytes 17109156 | tf_op jit(solution)/shard_map/myz,mn->nyz/dot_general | solution.py:82
  1501.1 187.4 %all_to_all.111 = f32[512,128,32]{1,2,0:T(8,128)} all-to-all(f32[512,128,32]{1,2,0:T(8,128)S(1)} %copy.99), channel_id=1, replica_groups=mesh['wide'=4,'narrow'=8] {'wide'}, dimensions={0} | all-to-all | bytes 16777216 | tf_op jit(solution)/shard_map/all_to_all | solution.py:132
  1688.5 12.2 copy.141
  1700.7 10.3 all_to_all.97
  1710.9 24.9 %convolution_bitcast_fusion = f32[128,512,32]{0,1,2:T(8,128)S(1)} fusion(f32[128,512,32]{1,0,2:T(8,128)} %all_to_all.97, s32[512]{0:T(512)S(1)} %multiply_add_fusion.2, f32[512]{0:T(512)S(1)} %broadcast_select_fusion), kind=kOutput, calls=%fused_computation.96 | convolution fusion | flops 12888834048 | bytes 16781312 | tf_op jit(solution)/shard_map/xmz,mn->xnz/dot_general | solution.py:82
  1749.1 11.6 copy.105
  1760.7 82.4 %all-to-all-done.5 = f32[128,512,32]{0,2,1:T(8,128)} async-done(((f32[128,512,32]{0,2,1:T(8,128)}), f32[128,512,32]{0,2,1:T(8,128)}, u32[]{:S(2)}, u32[]{:S(2)}) %all-to-all-start.5) | async-done | bytes 8388640 | tf_op jit(solution)/shard_map/all_to_all | solution.py:135
  1847.5 21.2 %multiply_reduce_fusion = (f32[]{:T(128)}, f32[128,64,256]{2,0,1:T(8,128)}) fusion(f32[128,64,256]{2,0,1:T(8,128)} %multiply_subtract_fusion, f32[128,64,256]{0,2,1:T(8,128)S(1)} %bitcast.179, s32[256]{0:T(256)S(1)} %multiply_add_fusion.3, f32[256]{0:T(256)S(1)} %compare_select_fusion.3), kind=kOutput, calls=%fused_computation.62 | convolution fusion | flops 6447628288 | bytes 25167876 | tf_op jit(solution)/shard_map/xym,mn->xyn/dot_general | solution.py:82
  1868.8 38.1 %psum.23 = f32[]{:T(128)} all-reduce(f32[]{:T(128)} %get-tuple-element.76), channel_id=1, replica_groups=mesh['wide'=4,'narrow'=8] {'wide','narrow'}, use_global_device_ids=true, to_apply=%region_6.7 | all-reduce | flops 1 | bytes 8 | tf_op jit(solution)/shard_map/psum | solution.py:170
  1908.2 13.9 multiply_add_fusion
  1922.1 11.6 copy.106
  (129 shorter events, 188.7 us)
Async XLA Ops:
  2.4 8.4 copy-start.6
  10.8 41.9 %copy-start.3 = (f32[128,64,256]{2,0,1:T(8,128)}, f32[128,64,256]{2,0,1:T(8,128)S(1)}, u32[]{:S(2)}) copy-start(f32[128,64,256]{2,0,1:T(8,128)S(1)} %copy.143) | copy-start | bytes 25165828
  24.9 27.9 %copy-start.2 = (f32[1,128,64,256]{3,1,2,0:T(8,128)}, f32[1,128,64,256]{3,1,2,0:T(8,128)S(1)}, u32[]{:S(2)}) copy-start(f32[1,128,64,256]{3,1,2,0:T(8,128)S(1)} %get-tuple-element.26) | copy-start | bytes 25165828
  39.2 13.5 copy-start.4
  39.5 9.1 collective-permute-start
  44.5 11.3 copy-start.13
  44.5 8.3 collective-permute-start.1
  52.8 3.6 collective-permute-start.2
  54.3 5.4 collective-permute-start.3
  102.5 6.1 copy-start.1
  223.4 3.4 copy-start.5
  229.5 18.4 collective-permute-start.4
  237.3 27.4 %collective-permute-start.5 = (f32[128,64,32]{0,2,1:T(8,128)}, f32[128,64,32]{0,2,1:T(8,128)}, u32[]{:S(2)}, u32[]{:S(2)}) collective-permute-start(f32[128,64,32]{0,2,1:T(8,128)} %get-tuple-element.57), channel_id=1, source_target_pairs={{0,2},{1,3},{2,4},{3,5},{4,6},{5,7},{6,0},{7,1},{8,10},{9,11},{10,... | collective-permute-start | bytes 3145736 | tf_op jit(solution)/shard_map/ppermute | solution.py:33
  238.8 62.3 %collective-permute-start.6 = (f32[128,64,32]{0,2,1:T(8,128)}, f32[128,64,32]{0,2,1:T(8,128)}, u32[]{:S(2)}, u32[]{:S(2)}) collective-permute-start(f32[128,64,32]{0,2,1:T(8,128)} %get-tuple-element.56), channel_id=1, source_target_pairs={{0,3},{1,4},{2,5},{3,6},{4,7},{5,0},{6,1},{7,2},{8,11},{9,12},{10,... | collective-permute-start | bytes 3145736 | tf_op jit(solution)/shard_map/ppermute | solution.py:33
  238.8 93.0 %copy-start.12 = (s32[1024]{0:T(1024)}, s32[1024]{0:T(1024)S(1)}, u32[]{:S(2)}) copy-start(s32[1024]{0:T(1024)S(1)} %pad_clamp_fusion) | copy-start | bytes 12292
  238.8 67.6 %collective-permute-start.7 = (f32[128,64,32]{0,2,1:T(8,128)}, f32[128,64,32]{0,2,1:T(8,128)S(1)}, u32[]{:S(2)}, u32[]{:S(2)}) collective-permute-start(f32[128,64,32]{0,2,1:T(8,128)} %get-tuple-element.55), channel_id=1, source_target_pairs={{0,4},{1,5},{2,6},{3,7},{4,0},{5,1},{6,2},{7,3},{8,12},{9,13},{10,... | collective-permute-start | bytes 3145736 | tf_op jit(solution)/shard_map/ppermute | solution.py:33
  240.2 90.6 %collective-permute-start.10 = (f32[128,64,32]{0,2,1:T(8,128)S(1)}, f32[128,64,32]{0,2,1:T(8,128)S(1)}, u32[]{:S(2)}, u32[]{:S(2)}) collective-permute-start(f32[128,64,32]{0,2,1:T(8,128)S(1)} %get-tuple-element.52), channel_id=1, source_target_pairs={{0,7},{1,0},{2,1},{3,2},{4,3},{5,4},{6,5},{7,6},{8,15},{9,8},{10,9... | collective-permute-start | bytes 3145736 | tf_op jit(solution)/shard_map/ppermute | solution.py:33
  247.9 80.8 %collective-permute-start.8 = (f32[128,64,32]{0,2,1:T(8,128)S(1)}, f32[128,64,32]{0,2,1:T(8,128)S(1)}, u32[]{:S(2)}, u32[]{:S(2)}) collective-permute-start(f32[128,64,32]{0,2,1:T(8,128)S(1)} %get-tuple-element.54), channel_id=1, source_target_pairs={{0,5},{1,6},{2,7},{3,0},{4,1},{5,2},{6,3},{7,4},{8,13},{9,14},{10,... | collective-permute-start | bytes 3145736 | tf_op jit(solution)/shard_map/ppermute | solution.py:33
  264.7 65.1 %collective-permute-start.9 = (f32[128,64,32]{0,2,1:T(8,128)S(1)}, f32[128,64,32]{0,2,1:T(8,128)S(1)}, u32[]{:S(2)}, u32[]{:S(2)}) collective-permute-start(f32[128,64,32]{0,2,1:T(8,128)S(1)} %get-tuple-element.53), channel_id=1, source_target_pairs={{0,6},{1,7},{2,0},{3,1},{4,2},{5,3},{6,4},{7,5},{8,14},{9,15},{10,... | collective-permute-start | bytes 3145736 | tf_op jit(solution)/shard_map/ppermute | solution.py:33
  380.0 5.7 copy-start.11
  380.0 190.0 %all-to-all-start = ((f32[128,512,32]{0,2,1:T(8,128)}), f32[128,512,32]{0,2,1:T(8,128)}, u32[]{:S(2)}, u32[]{:S(2)}) async-start(f32[128,512,32]{0,2,1:T(8,128)} %copy.82), calls=%async_computation | async-start | bytes 16777216 | tf_op jit(solution)/shard_map/all_to_all | solution.py:122
  387.0 215.6 %copy-start.14 = (f32[32]{0:T(128)}, f32[32]{0:T(128)S(1)}, u32[]{:S(2)}) copy-start(f32[32]{0:T(128)S(1)} %multiply_subtract_fusion.2) | copy-start | bytes 388
  387.1 215.6 %copy-start.16 = (pred[32]{0:T(512)(128)(4,1)}, pred[32]{0:T(512)(128)(4,1)S(1)}, u32[]{:S(2)}) copy-start(pred[32]{0:T(512)(128)(4,1)S(1)} %fusion.171) | copy-start | bytes 100
  387.3 215.3 %copy-start.9 = (pred[512,128]{1,0:T(8,128)(4,1)}, pred[512,128]{1,0:T(8,128)(4,1)S(1)}, u32[]{:S(2)}) copy-start(pred[512,128]{1,0:T(8,128)(4,1)S(1)} %broadcast_and_fusion) | copy-start | bytes 196612
  387.5 215.2 %copy-start.7 = (f32[512,128]{1,0:T(8,128)}, f32[512,128]{1,0:T(8,128)S(1)}, u32[]{:S(2)}) copy-start(f32[512,128]{1,0:T(8,128)S(1)} %broadcast_add_fusion) | copy-start | bytes 786436
  987.1 32.8 %copy-start = (f32[128,64,256]{2,0,1:T(8,128)}, f32[128,64,256]{2,0,1:T(8,128)S(1)}, u32[]{:S(2)}) copy-start(f32[128,64,256]{2,0,1:T(8,128)S(1)} %fusion.129) | copy-start | bytes 25165828
  987.2 14.0 collective-permute-start.12
  989.0 12.1 collective-permute-start.11
  1001.2 11.6 collective-permute-start.13
  1002.5 10.3 collective-permute-start.14
  1113.3 25.9 %collective-permute-start.15 = (f32[128,64,32]{0,2,1:T(8,128)S(1)}, f32[128,64,32]{0,2,1:T(8,128)S(1)}, u32[]{:S(2)}, u32[]{:S(2)}) collective-permute-start(f32[128,64,32]{0,2,1:T(8,128)S(1)} %get-tuple-element.49), channel_id=1, source_target_pairs={{0,1},{1,2},{2,3},{3,4},{4,5},{5,6},{6,7},{7,0},{8,9},{9,10},{10,1... | collective-permute-start | bytes 3145736 | tf_op jit(solution)/shard_map/ppermute | solution.py:33
  1113.4 27.0 %collective-permute-start.16 = (f32[128,64,32]{0,2,1:T(8,128)S(1)}, f32[128,64,32]{0,2,1:T(8,128)S(1)}, u32[]{:S(2)}, u32[]{:S(2)}) collective-permute-start(f32[128,64,32]{0,2,1:T(8,128)S(1)} %get-tuple-element.48), channel_id=1, source_target_pairs={{0,2},{1,3},{2,4},{3,5},{4,6},{5,7},{6,0},{7,1},{8,10},{9,11},{10,... | collective-permute-start | bytes 3145736 | tf_op jit(solution)/shard_map/ppermute | solution.py:33
  1115.7 68.9 %collective-permute-start.17 = (f32[128,64,32]{0,2,1:T(8,128)S(1)}, f32[128,64,32]{0,2,1:T(8,128)S(1)}, u32[]{:S(2)}, u32[]{:S(2)}) collective-permute-start(f32[128,64,32]{0,2,1:T(8,128)S(1)} %get-tuple-element.47), channel_id=1, source_target_pairs={{0,3},{1,4},{2,5},{3,6},{4,7},{5,0},{6,1},{7,2},{8,11},{9,12},{10,... | collective-permute-start | bytes 3145736 | tf_op jit(solution)/shard_map/ppermute | solution.py:33
  1117.3 68.3 %collective-permute-start.18 = (f32[128,64,32]{0,2,1:T(8,128)S(1)}, f32[128,64,32]{0,2,1:T(8,128)S(1)}, u32[]{:S(2)}, u32[]{:S(2)}) collective-permute-start(f32[128,64,32]{0,2,1:T(8,128)S(1)} %get-tuple-element.46), channel_id=1, source_target_pairs={{0,4},{1,5},{2,6},{3,7},{4,0},{5,1},{6,2},{7,3},{8,12},{9,13},{10,... | collective-permute-start | bytes 3145736 | tf_op jit(solution)/shard_map/ppermute | solution.py:33
  1118.5 90.7 %collective-permute-start.21 = (f32[128,64,32]{0,2,1:T(8,128)S(1)}, f32[128,64,32]{0,2,1:T(8,128)S(1)}, u32[]{:S(2)}, u32[]{:S(2)}) collective-permute-start(f32[128,64,32]{0,2,1:T(8,128)S(1)} %get-tuple-element.43), channel_id=1, source_target_pairs={{0,7},{1,0},{2,1},{3,2},{4,3},{5,4},{6,5},{7,6},{8,15},{9,8},{10,9... | collective-permute-start | bytes 3145736 | tf_op jit(solution)/shard_map/ppermute | solution.py:33
  1139.2 67.9 %collective-permute-start.19 = (f32[128,64,32]{0,2,1:T(8,128)S(1)}, f32[128,64,32]{0,2,1:T(8,128)S(1)}, u32[]{:S(2)}, u32[]{:S(2)}) collective-permute-start(f32[128,64,32]{0,2,1:T(8,128)S(1)} %get-tuple-element.45), channel_id=1, source_target_pairs={{0,5},{1,6},{2,7},{3,0},{4,1},{5,2},{6,3},{7,4},{8,13},{9,14},{10,... | collective-permute-start | bytes 3145736 | tf_op jit(solution)/shard_map/ppermute | solution.py:33
  1140.4 67.8 %collective-permute-start.20 = (f32[128,64,32]{0,2,1:T(8,128)S(1)}, f32[128,64,32]{0,2,1:T(8,128)S(1)}, u32[]{:S(2)}, u32[]{:S(2)}) collective-permute-start(f32[128,64,32]{0,2,1:T(8,128)S(1)} %get-tuple-element.44), channel_id=1, source_target_pairs={{0,6},{1,7},{2,0},{3,1},{4,2},{5,3},{6,4},{7,5},{8,14},{9,15},{10,... | collective-permute-start | bytes 3145736 | tf_op jit(solution)/shard_map/ppermute | solution.py:33
  1453.6 22.5 %copy-start.8 = (f32[512,128]{1,0:T(8,128)S(1)}, f32[512,128]{1,0:T(8,128)}, u32[]{:S(2)}) copy-start(f32[512,128]{1,0:T(8,128)} %copy-done.7) | copy-start | bytes 786436
  1453.6 22.6 %copy-start.10 = (pred[512,128]{1,0:T(8,128)(4,1)S(1)}, pred[512,128]{1,0:T(8,128)(4,1)}, u32[]{:S(2)}) copy-start(pred[512,128]{1,0:T(8,128)(4,1)} %copy-done.9) | copy-start | bytes 196612
  1453.6 22.6 %copy-start.15 = (f32[32]{0:T(128)S(1)}, f32[32]{0:T(128)}, u32[]{:S(2)}) copy-start(f32[32]{0:T(128)} %copy-done.14) | copy-start | bytes 388
  1453.6 22.6 %copy-start.17 = (pred[32]{0:T(512)(128)(4,1)S(1)}, pred[32]{0:T(512)(128)(4,1)}, u32[]{:S(2)}) copy-start(pred[32]{0:T(512)(128)(4,1)} %copy-done.16) | copy-start | bytes 100
  1744.1 99.0 %all-to-all-start.5 = ((f32[128,512,32]{0,2,1:T(8,128)}), f32[128,512,32]{0,2,1:T(8,128)}, u32[]{:S(2)}, u32[]{:S(2)}) async-start(f32[128,512,32]{0,2,1:T(8,128)} %copy.101), calls=%async_computation.5 | async-start | bytes 16777216 | tf_op jit(solution)/shard_map/all_to_all | solution.py:135
